TPU v7x, 32 devices: a whole 2x2x4 slice. The times are simulated.
32 devices in a mesh: row: 4 (over z), col: 8 (over y, x, core).
Axes of the slice: x: 2, y: 2, z: 4, core: 2. Of those that a mesh axis runs over, the one named last changes fastest.
Arguments:
- right_side: float32 [2, 16, 512, 512], P(None, None, 'row', 'col'), may hold values from -12 to 12
- symbol: float32 [1024, 1024, 256], P('col', 'row'), may hold values from -0.25 to 4.75, as said below
Outputs:
- solution_field: float32 [2, 16, 512, 512], P(None, None, 'row', 'col')
- residual: float32 [2, 16, 512, 512], P(None, None, 'row', 'col')
Inputs may be any that keep to these rules, and one draw needn't show every extreme that they name: For each frequency pair (u, v) the 16 x 16 matrix with entries symbol[u, v, s * 16 + t] is symmetric and positive definite.
All inputs are finite; a program needn't handle non-finite values.
Results may differ from a plain program's by a relative error of at most 0.0003.
Values sent between devices are 32-bit elements; how exact they have to be, the bound alone decides.
A program may use at most 576 MiB of HBM per device.

v0:
```python
import math
import jax
import jax.numpy as jnp
from jax import lax
from jax.sharding import PartitionSpec as P

precise = lax.Precision.HIGHEST


def twiddle(out_index, in_index, length):
    product = out_index[:, None] * in_index[None, :] % length
    angle = product.astype(jnp.float32) * (2.0 * math.pi / length)
    return (jnp.cos(angle), jnp.sin(angle))


def widen(values):
    return values[:, None, None, None]


def squares(residual):
    return lax.psum(jnp.sum(residual * residual, axis=(1, 2, 3)), ("row", "col"))


def local(right_side, symbol):
    row_count = lax.axis_size("row")
    col_count = lax.axis_size("col")
    rhs_count, seg_count, row_block, col_block = right_side.shape
    rows_all = row_block * row_count
    cols_all = col_block * col_count
    freq_rows = 2 * rows_all
    freq_cols = 2 * cols_all
    blocks = symbol.reshape(symbol.shape[0], symbol.shape[1], seg_count, seg_count)
    rows_cos, rows_sin = twiddle(
        jnp.arange(freq_rows, dtype=jnp.int32), jnp.arange(rows_all, dtype=jnp.int32), freq_rows
    )
    cols_cos, cols_sin = twiddle(
        jnp.arange(freq_cols, dtype=jnp.int32), jnp.arange(cols_all, dtype=jnp.int32), freq_cols
    )
    back_cols_cos, back_cols_sin = (cols_cos.T, cols_sin.T)
    back_rows_cos, back_rows_sin = (rows_cos.T, rows_sin.T)
    norm_factor = 1.0 / (freq_rows * freq_cols)
    residual = right_side
    norm_now = squares(residual)
    whole_rows = lax.all_to_all(right_side, "row", split_axis=1, concat_axis=2, tiled=True)
    real_rows = jnp.einsum("ui,ksij->ksuj", rows_cos, whole_rows, precision=precise)
    imag_rows = -jnp.einsum("ui,ksij->ksuj", rows_sin, whole_rows, precision=precise)
    whole_cols = lax.all_to_all(
        jnp.stack([real_rows, imag_rows]), "col", split_axis=3, concat_axis=4, tiled=True
    )
    cos_part = jnp.einsum("vj,rksuj->rksuv", cols_cos, whole_cols, precision=precise)
    sin_part = jnp.einsum("vj,rksuj->rksuv", cols_sin, whole_cols, precision=precise)
    spectrum = jnp.stack([cos_part[0] + sin_part[1], cos_part[1] - sin_part[0]])
    all_segments = lax.all_to_all(spectrum, "row", split_axis=4, concat_axis=2, tiled=True)
    mixture = jnp.einsum("uvst,rktuv->rksuv", blocks, all_segments, precision=precise)
    own_segments = lax.all_to_all(mixture, "row", split_axis=2, concat_axis=4, tiled=True)
    cos_back = jnp.einsum("jv,rksuv->rksuj", back_cols_cos, own_segments, precision=precise)
    sin_back = jnp.einsum("jv,rksuv->rksuj", back_cols_sin, own_segments, precision=precise)
    inverted = jnp.stack([cos_back[0] - sin_back[1], sin_back[0] + cos_back[1]])
    freq_whole = lax.all_to_all(inverted, "col", split_axis=4, concat_axis=3, tiled=True)
    spatial = jnp.einsum("iu,ksuj->ksij", back_rows_cos, freq_whole[0], precision=precise)
    spatial = (
        spatial - jnp.einsum("iu,ksuj->ksij", back_rows_sin, freq_whole[1], precision=precise)
    ) * norm_factor
    returned = lax.all_to_all(spatial, "row", split_axis=2, concat_axis=1, tiled=True)
    curve = lax.psum(jnp.sum(right_side * returned, axis=(1, 2, 3)), ("row", "col"))
    step_size = widen(norm_now / curve)
    solution = step_size * right_side
    residual = residual - step_size * returned
    return (solution, residual)


def solution(mesh):
    placed = (P(None, None, "row", "col"), P("col", "row", None))
    return jax.shard_map(
        local,
        mesh=mesh,
        in_specs=placed,
        out_specs=(P(None, None, "row", "col"), P(None, None, "row", "col")),
        check_vma=False,
    )
```

profile of v0, /device:TPU:0, one launch (start us, length us, event | category | flops | bytes accessed | tf_op | source)
XLA Modules:
  0.0 1495.4 jit_solution(2727610797402067509)
XLA Ops:
  2.0 31.9 %all_to_all.105 = f32[2,16,128,64]{2,3,0,1:T(8,128)S(1)} all-to-all(f32[2,16,128,64]{2,3,0,1:T(8,128)S(1)} %copy.43), channel_id=1, replica_groups=mesh['row'=4,'col'=8] {'row'}, dimensions={1} | all-to-all | bytes 2097152 | tf_op jit(solution)/shard_map/all_to_all | solution.py:44
  34.9 12.5 negate_bitcast_fusion
  47.5 12.7 fusion.24
  71.0 11.5 reshape.18
  82.5 53.7 %all_to_all.106 = f32[8,1,131072]{2,1,0:T(1,128)} all-to-all(f32[8,1,131072]{2,1,0:T(1,128)} %reshape.18), channel_id=1, replica_groups=mesh['row'=4,'col'=8] {'col'}, dimensions={0} | all-to-all | bytes 8388608 | tf_op jit(solution)/shard_map/all_to_all | solution.py:47
  136.8 13.7 reduce
  150.5 11.1 reshape.19
  170.1 38.7 %fusion.17 = f32[2,2,4,128,1024]{4,3,2,1,0:T(8,128)} fusion(f32[2,2,4,128,512]{3,4,2,1,0:T(8,128)} %bitcast.111), kind=kOutput, calls=%fused_computation.28 | convolution fusion | flops 12892241920 | bytes 12582912 | tf_op jit(solution)/shard_map/vj,rksuj->rksuv/dot_general | solution.py:51
  208.9 36.0 %fusion.5 = f32[2,2,4,128,1024]{4,3,2,1,0:T(8,128)} fusion(f32[2,2,4,128,512]{3,4,2,1,0:T(8,128)S(1)} %bitcast.112), kind=kOutput, calls=%fused_computation.16 | convolution fusion | flops 12892241920 | bytes 12582912 | tf_op jit(solution)/shard_map/vj,rksuj->rksuv/dot_general | solution.py:50
  277.7 33.5 %copy.53 = f32[128,256,256]{1,2,0:T(8,128)} copy(f32[128,256,256]{2,1,0:T(8,128)} %param.3) | data formatting | bytes 67108864 | tf_op args[1]
  311.2 124.5 %copy.71 = f32[128,256,16,16,1]{3,2,4,1,0:T(8,128)} copy(f32[128,256,16,16,1]{1,3,2,0,4:T(8,128)} %bitcast.100) | data formatting | bytes 67108864 | tf_op jit(solution)/shard_map/reshape | solution.py:32
  435.6 24.8 %all-to-all-done.2 = f32[2,2,4,128,1024]{3,2,1,0,4:T(4,128)} async-done(((f32[2,2,4,128,1024]{3,2,1,0,4:T(4,128)}), f32[2,2,4,128,1024]{3,2,1,0,4:T(4,128)}, u32[]{:S(2)}, u32[]{:S(2)}) %all-to-all-start.2) | async-done | bytes 8388640 | tf_op jit(solution)/shard_map/all_to_all | solution.py:53
  479.7 52.4 %copy.54 = f32[2,2,16,128,256]{2,1,0,4,3:T(2,128)} copy(f32[2,2,16,128,256]{4,3,2,1,0:T(8,128)} %bitcast.101) | data formatting | bytes 16777216 | tf_op jit(solution)/shard_map/all_to_all | solution.py:53
  532.1 443.6 %convolution_bitcast_fusion = f32[2,2,16,128,256]{2,1,0,4,3:T(2,128)} fusion(f32[2,2,16,128,256]{2,1,0,4,3:T(2,128)} %copy.54, f32[128,256,16,16,1]{3,2,4,1,0:T(8,128)} %copy.71), kind=kOutput, calls=%fused_computation | convolution fusion | flops 402653184 | bytes 50331648 | tf_op jit(solution)/shard_map/uvst,rktuv->rksuv/dot_general | solution.py:54
  975.7 54.4 %copy.56 = f32[2,2,16,128,256]{4,3,1,0,2:T(8,128)} copy(f32[2,2,16,128,256]{2,1,0,4,3:T(2,128)} %convolution_bitcast_fusion) | data formatting | bytes 16777216 | tf_op jit(solution)/shard_map/uvst,rktuv->rksuv/transpose | solution.py:54
  1030.1 190.1 %all_to_all.107 = f32[2,2,16,128,256]{4,3,1,0,2:T(8,128)} all-to-all(f32[2,2,16,128,256]{4,3,1,0,2:T(8,128)} %copy.56), channel_id=1, replica_groups=mesh['row'=4,'col'=8] {'row'}, dimensions={2} | all-to-all | bytes 16777216 | tf_op jit(solution)/shard_map/all_to_all | solution.py:55
  1220.2 12.2 copy.58
  1243.1 52.4 %fusion.15 = f32[2,2,4,128,512]{4,3,2,1,0:T(8,128)S(1)} fusion(f32[2,2,4,128,1024]{4,3,2,1,0:T(8,128)} %all_to_all.91), kind=kOutput, calls=%fused_computation.26 | convolution fusion | flops 12892241920 | bytes 12582912 | tf_op jit(solution)/shard_map/jv,rksuv->rksuj/dot_general | solution.py:57
  1295.5 22.5 %fusion.3 = f32[2,2,4,128,512]{4,3,2,1,0:T(8,128)S(1)} fusion(f32[2,2,4,128,1024]{4,3,2,1,0:T(8,128)S(1)} %copy-done.1), kind=kOutput, calls=%fused_computation.14 | convolution fusion | flops 12892241920 | bytes 12582912 | tf_op jit(solution)/shard_map/jv,rksuv->rksuj/dot_general | solution.py:56
  1326.9 52.9 %all_to_all.108 = f32[2,2,4,128,512]{3,2,1,0,4:T(4,128)S(1)} all-to-all(f32[2,2,4,128,512]{3,2,1,0,4:T(4,128)} %copy.59), channel_id=1, replica_groups=mesh['row'=4,'col'=8] {'col'}, dimensions={4} | all-to-all | bytes 8388608 | tf_op jit(solution)/shard_map/all_to_all | solution.py:59
  1389.8 13.4 fusion.7
  1403.3 12.0 fusion.33
  1418.4 28.1 %all_to_all.109 = f32[4,1,65536]{2,1,0:T(1,128)S(1)} all-to-all(f32[4,1,65536]{2,1,0:T(1,128)S(1)} %reshape.20), channel_id=1, replica_groups=mesh['row'=4,'col'=8] {'row'}, dimensions={0} | all-to-all | bytes 2097152 | tf_op jit(solution)/shard_map/all_to_all | solution.py:64
  1455.4 37.8 %all-reduce = (f32[2]{0:T(128)S(1)}, f32[2]{0:T(128)S(1)}) all-reduce(f32[2]{0:T(128)S(1)} %get-tuple-element.3, f32[2]{0:T(128)S(1)} %get-tuple-element.2), channel_id=1, replica_groups=mesh['row'=4,'col'=8] {'row','col'}, use_global_device_ids=true, to_apply=%region_1.2 | all-reduce | flops 4 | bytes 32 | tf_op jit(solution)/shard_map/psum | solution.py:21
  (39 shorter events, 117.5 us)
Async XLA Ops:
  170.1 38.8 %copy-start.2 = (f32[2,2,4,8,128,64]{4,5,3,2,1,0:T(8,128)S(1)}, f32[2,2,4,8,128,64]{4,5,3,2,1,0:T(8,128)}, u32[]{:S(2)}) copy-start(f32[2,2,4,8,128,64]{4,5,3,2,1,0:T(8,128)} %copy.73) | copy-start | bytes 12582916
  272.1 188.4 %all-to-all-start.2 = ((f32[2,2,4,128,1024]{3,2,1,0,4:T(4,128)}), f32[2,2,4,128,1024]{3,2,1,0,4:T(4,128)}, u32[]{:S(2)}, u32[]{:S(2)}) async-start(f32[2,2,4,128,1024]{3,2,1,0,4:T(4,128)} %copy.50), calls=%async_computation.2 | async-start | bytes 16777216 | tf_op jit(solution)/shard_map/all_to_all | solution.py:53
  1243.1 52.5 %copy-start.1 = (f32[2,2,4,128,1024]{4,3,2,1,0:T(8,128)S(1)}, f32[2,2,4,128,1024]{4,3,2,1,0:T(8,128)}, u32[]{:S(2)}) copy-start(f32[2,2,4,128,1024]{4,3,2,1,0:T(8,128)} %all_to_all.91) | copy-start | bytes 25165828
  1389.8 13.4 copy-start.3
  1453.1 2.0 copy-start
where the time goes:
time: 1510 us; the launch traced here: 1500 us
  matrix products  644 us (43%)
  blocking collectives  395 us (26%)
  local copies, waits for them, and re-layouts  383 us (25%)
  other arithmetic  42 us (3%)
  waiting for transfers between devices  24.8 us (2%)
    dot_general x1, matrix products, local(): jnp.einsum('uvst,rktuv->rksuv', blocks, all_segments, precision=precise)  444 us
    all_to_all x1, blocking collectives, local(): lax.all_to_all(mixture, 'row', split_axis=2, concat_axis=4, tiled=True)  190 us
    reshape x1, local copies, waits for them, and re-layouts, local(): symbol.reshape(symbol.shape[0], symbol.shape[1], seg_count, seg_count)  124 us
    all_to_all x3, local copies, waits for them, and re-layouts, local(): lax.all_to_all(spectrum, 'row', split_axis=4, concat_axis=2, tiled=True)  71.6 us
    unnamed x14, local copies, waits for them, and re-layouts  62.3 us
    transpose x1, local copies, waits for them, and re-layouts, local(): jnp.einsum('uvst,rktuv->rksuv', blocks, all_segments, precision=precise)  54.4 us
    all_to_all x1, blocking collectives, local(): lax.all_to_all(jnp.stack([real_rows, imag_rows]), 'col', split_axis=3, co...  53.7 us
    all_to_all x1, blocking collectives, local(): lax.all_to_all(inverted, 'col', split_axis=4, concat_axis=3, tiled=True)  52.9 us
  transfers between devices with their start and end apart: 1, of which 1 were waited for; matrix products, arithmetic and copies ran while one was open for 11% of the time, Pallas kernels for 0%

commit v1 on v0

--- a/solution.py
+++ b/solution.py
@@ -44,9 +44,10 @@
     whole_rows = lax.all_to_all(right_side, "row", split_axis=1, concat_axis=2, tiled=True)
     real_rows = jnp.einsum("ui,ksij->ksuj", rows_cos, whole_rows, precision=precise)
     imag_rows = -jnp.einsum("ui,ksij->ksuj", rows_sin, whole_rows, precision=precise)
-    whole_cols = lax.all_to_all(
-        jnp.stack([real_rows, imag_rows]), "col", split_axis=3, concat_axis=4, tiled=True
-    )
+    own = jnp.stack([real_rows, imag_rows])
+    pieces = jnp.split(own, lax.axis_size("col"), axis=3)
+    received = lax.all_to_all(jnp.stack(pieces), "col", 0, 0)
+    whole_cols = jnp.concatenate(received, axis=4)
     cos_part = jnp.einsum("vj,rksuj->rksuv", cols_cos, whole_cols, precision=precise)
     sin_part = jnp.einsum("vj,rksuj->rksuv", cols_sin, whole_cols, precision=precise)
     spectrum = jnp.stack([cos_part[0] + sin_part[1], cos_part[1] - sin_part[0]])

time: 1510 us -> 1460 us (0.967)
  local copies, waits for them, and re-layouts: 383 us -> 342 us
  other arithmetic: 42 us -> 26.5 us
    unnamed x14 -> x10, local copies, waits for them, and re-layouts: 62.3 us -> 39.6 us
where the time goes in v1:
time: 1460 us; the launch traced here: 1450 us
  matrix products  655 us (45%)
  blocking collectives  393 us (27%)
  local copies, waits for them, and re-layouts  342 us (23%)
  other arithmetic  26.5 us (2%)
  waiting for transfers between devices  24.9 us (2%)
    dot_general x1, matrix products, local(): jnp.einsum('uvst,rktuv->rksuv', blocks, all_segments, precision=precise)  444 us
    all_to_all x1, blocking collectives, local(): lax.all_to_all(mixture, 'row', split_axis=2, concat_axis=4, tiled=True)  190 us
    reshape x1, local copies, waits for them, and re-layouts, local(): symbol.reshape(symbol.shape[0], symbol.shape[1], seg_count, seg_count)  124 us
    all_to_all x3, local copies, waits for them, and re-layouts, local(): lax.all_to_all(spectrum, 'row', split_axis=4, concat_axis=2, tiled=True)  71.6 us
    transpose x1, local copies, waits for them, and re-layouts, local(): jnp.einsum('uvst,rktuv->rksuv', blocks, all_segments, precision=precise)  54.4 us
    all_to_all x1, blocking collectives, local(): lax.all_to_all(inverted, 'col', split_axis=4, concat_axis=3, tiled=True)  52.9 us
    all_to_all x1, blocking collectives, local(): received = lax.all_to_all(jnp.stack(pieces), 'col', 0, 0)  52.6 us
    dot_general x1, matrix products, local(): jnp.einsum('jv,rksuv->rksuj', back_cols_sin, own_segments, precision=prec...  52.4 us
  transfers between devices with their start and end apart: 1, of which 1 were waited for; matrix products, arithmetic and copies ran while one was open for 11% of the time, Pallas kernels for 0%

profile of v1, /device:TPU:0, one launch (start us, length us, event | category | flops | bytes accessed | tf_op | source)
XLA Modules:
  0.0 1449.4 jit_solution(6859956753004009674)
XLA Ops:
  2.0 31.9 %all_to_all.92 = f32[2,16,128,64]{2,3,0,1:T(8,128)S(1)} all-to-all(f32[2,16,128,64]{2,3,0,1:T(8,128)S(1)} %copy.42), channel_id=1, replica_groups=mesh['row'=4,'col'=8] {'row'}, dimensions={1} | all-to-all | bytes 2097152 | tf_op jit(solution)/shard_map/all_to_all | solution.py:44
  34.9 12.7 fusion.24
  47.7 12.5 negate_bitcast_fusion
  60.8 52.6 %all_to_all.93 = f32[8,2,2,4,128,64]{4,5,3,2,1,0:T(8,128)S(1)} all-to-all(f32[8,2,2,4,128,64]{4,5,3,2,1,0:T(8,128)S(1)} %fusion.68), channel_id=1, replica_groups=mesh['row'=4,'col'=8] {'col'}, dimensions={0} | all-to-all | bytes 8388608 | tf_op jit(solution)/shard_map/all_to_all | solution.py:49
  114.0 48.0 %fusion.17 = f32[2,2,4,128,1024]{4,3,2,1,0:T(8,128)} fusion(f32[2,2,4,128,512]{3,4,2,1,0:T(8,128)S(1)} %bitcast.137), kind=kOutput, calls=%fused_computation.41 | convolution fusion | flops 12892241920 | bytes 12582912 | tf_op jit(solution)/shard_map/vj,rksuj->rksuv/dot_general | solution.py:52
  162.0 36.0 %fusion.5 = f32[2,2,4,128,1024]{4,3,2,1,0:T(8,128)} fusion(f32[2,2,4,128,512]{3,4,2,1,0:T(8,128)S(1)} %bitcast.138), kind=kOutput, calls=%fused_computation.29 | convolution fusion | flops 12892241920 | bytes 12582912 | tf_op jit(solution)/shard_map/vj,rksuj->rksuv/dot_general | solution.py:51
  198.0 10.3 slice_add_fusion
  214.9 10.2 copy.47
  230.8 33.5 %copy.50 = f32[128,256,256]{1,2,0:T(8,128)} copy(f32[128,256,256]{2,1,0:T(8,128)} %param.3) | data formatting | bytes 67108864 | tf_op args[1]
  264.2 124.5 %copy.68 = f32[128,256,16,16,1]{3,2,4,1,0:T(8,128)} copy(f32[128,256,16,16,1]{1,3,2,0,4:T(8,128)} %bitcast.127) | data formatting | bytes 67108864 | tf_op jit(solution)/shard_map/reshape | solution.py:32
  388.7 24.9 %all-to-all-done.2 = f32[2,2,4,128,1024]{3,2,1,0,4:T(4,128)} async-done(((f32[2,2,4,128,1024]{3,2,1,0,4:T(4,128)}), f32[2,2,4,128,1024]{3,2,1,0,4:T(4,128)}, u32[]{:S(2)}, u32[]{:S(2)}) %all-to-all-start.2) | async-done | bytes 8388640 | tf_op jit(solution)/shard_map/all_to_all | solution.py:54
  432.8 52.4 %copy.51 = f32[2,2,16,128,256]{2,1,0,4,3:T(2,128)} copy(f32[2,2,16,128,256]{4,3,2,1,0:T(8,128)} %bitcast.128) | data formatting | bytes 16777216 | tf_op jit(solution)/shard_map/all_to_all | solution.py:54
  485.2 443.6 %convolution_bitcast_fusion = f32[2,2,16,128,256]{2,1,0,4,3:T(2,128)} fusion(f32[2,2,16,128,256]{2,1,0,4,3:T(2,128)} %copy.51, f32[128,256,16,16,1]{3,2,4,1,0:T(8,128)} %copy.68), kind=kOutput, calls=%fused_computation | convolution fusion | flops 402653184 | bytes 50331648 | tf_op jit(solution)/shard_map/uvst,rktuv->rksuv/dot_general | solution.py:55
  928.8 54.4 %copy.53 = f32[2,2,16,128,256]{4,3,1,0,2:T(8,128)} copy(f32[2,2,16,128,256]{2,1,0,4,3:T(2,128)} %convolution_bitcast_fusion) | data formatting | bytes 16777216 | tf_op jit(solution)/shard_map/uvst,rktuv->rksuv/transpose | solution.py:55
  983.1 190.1 %all_to_all.94 = f32[2,2,16,128,256]{4,3,1,0,2:T(8,128)} all-to-all(f32[2,2,16,128,256]{4,3,1,0,2:T(8,128)} %copy.53), channel_id=1, replica_groups=mesh['row'=4,'col'=8] {'row'}, dimensions={2} | all-to-all | bytes 16777216 | tf_op jit(solution)/shard_map/all_to_all | solution.py:56
  1173.2 12.2 copy.55
  1185.4 10.7 all_to_all.78
  1196.2 52.4 %fusion.15 = f32[2,2,4,128,512]{4,3,2,1,0:T(8,128)S(1)} fusion(f32[2,2,4,128,1024]{4,3,2,1,0:T(8,128)} %all_to_all.78), kind=kOutput, calls=%fused_computation.39 | convolution fusion | flops 12892241920 | bytes 12582912 | tf_op jit(solution)/shard_map/jv,rksuv->rksuj/dot_general | solution.py:58
  1248.6 22.5 %fusion.3 = f32[2,2,4,128,512]{4,3,2,1,0:T(8,128)S(1)} fusion(f32[2,2,4,128,1024]{4,3,2,1,0:T(8,128)S(1)} %copy-done.1), kind=kOutput, calls=%fused_computation.27 | convolution fusion | flops 12892241920 | bytes 12582912 | tf_op jit(solution)/shard_map/jv,rksuv->rksuj/dot_general | solution.py:57
  1280.0 52.9 %all_to_all.95 = f32[2,2,4,128,512]{3,2,1,0,4:T(4,128)S(1)} all-to-all(f32[2,2,4,128,512]{3,2,1,0,4:T(4,128)} %copy.56), channel_id=1, replica_groups=mesh['row'=4,'col'=8] {'col'}, dimensions={4} | all-to-all | bytes 8388608 | tf_op jit(solution)/shard_map/all_to_all | solution.py:60
  1338.7 13.7 fusion.7
  1355.1 13.7 fusion.33
  1372.0 28.1 %all_to_all.96 = f32[4,1,65536]{2,1,0:T(1,128)S(1)} all-to-all(f32[4,1,65536]{2,1,0:T(1,128)S(1)} %reshape.26), channel_id=1, replica_groups=mesh['row'=4,'col'=8] {'row'}, dimensions={0} | all-to-all | bytes 2097152 | tf_op jit(solution)/shard_map/all_to_all | solution.py:65
  1409.5 37.8 %all-reduce = (f32[2]{0:T(128)S(1)}, f32[2]{0:T(128)S(1)}) all-reduce(f32[2]{0:T(128)S(1)} %get-tuple-element.3, f32[2]{0:T(128)S(1)} %get-tuple-element.2), channel_id=1, replica_groups=mesh['row'=4,'col'=8] {'row','col'}, use_global_device_ids=true, to_apply=%region_1.2 | all-reduce | flops 4 | bytes 32 | tf_op jit(solution)/shard_map/psum | solution.py:21
  (40 shorter events, 66.5 us)
Async XLA Ops:
  225.2 188.4 %all-to-all-start.2 = ((f32[2,2,4,128,1024]{3,2,1,0,4:T(4,128)}), f32[2,2,4,128,1024]{3,2,1,0,4:T(4,128)}, u32[]{:S(2)}, u32[]{:S(2)}) async-start(f32[2,2,4,128,1024]{3,2,1,0,4:T(4,128)} %copy.47), calls=%async_computation.2 | async-start | bytes 16777216 | tf_op jit(solution)/shard_map/all_to_all | solution.py:54
  1196.2 52.5 %copy-start.1 = (f32[2,2,4,128,1024]{4,3,2,1,0:T(8,128)S(1)}, f32[2,2,4,128,1024]{4,3,2,1,0:T(8,128)}, u32[]{:S(2)}) copy-start(f32[2,2,4,128,1024]{4,3,2,1,0:T(8,128)} %all_to_all.78) | copy-start | bytes 25165828
  1338.7 13.7 copy-start.2
  1407.1 2.0 copy-start
